TPU v7x, 32 devices: a whole 2x2x4 slice. The times are simulated.
32 devices in a mesh: dp: 8 (over y, x, core), tensor: 4 (over z).
Axes of the slice: x: 2, y: 2, z: 4, core: 2. Of those that a mesh axis runs over, the one named last changes fastest.
Arguments:
- tokens: bfloat16 [16384, 2048], P(('dp', 'tensor'))
- teacher: bfloat16 [16384, 2048], P(('dp', 'tensor')), may hold values from -6 to 6
- valid: int32 [16384], P(('dp', 'tensor')), may hold values from 0 to 1, as said below
- prefix: int32 [16], P('dp'), may hold values from 102 to 512, as said below
- w_query: bfloat16 [2048, 1024], P(None, 'tensor'), may hold values from -0.125 to 0.125
- key_weight: bfloat16 [2048, 256], replicated, may hold values from -0.125 to 0.125
- value_weight: bfloat16 [2048, 256], replicated, may hold values from -0.125 to 0.125
- query_gain: float32 [64], replicated, may hold values from 0.25 to 1.75
- key_gain: float32 [64], replicated, may hold values from 0.25 to 1.75
- w_out: bfloat16 [1024, 2048], P('tensor'), may hold values from -3 to 3
- attn_gain: float32 [2048], replicated, may hold values from 0.25 to 1.75
- ffn_gain: float32 [2048], replicated, may hold values from 0.25 to 1.75
- w_gate: bfloat16 [2048, 5120], P(None, 'tensor'), may hold values from -0.125 to 0.125
- w_up: bfloat16 [2048, 5120], P(None, 'tensor'), may hold values from -0.125 to 0.125
- w_down: bfloat16 [5120, 2048], P('tensor'), may hold values from -0.078125 to 0.078125
Outputs:
- output: bfloat16 [16384, 2048], P(('dp', 'tensor'))
- loss: float32 [], replicated
- grad_tokens: float32 [16384, 2048], P(('dp', 'tensor'))
- grad_query: float32 [2048, 1024], P(None, 'tensor')
- grad_key: float32 [2048, 256], replicated
- grad_value: float32 [2048, 256], replicated
- grad_query_gain: float32 [64], replicated
- grad_key_gain: float32 [64], replicated
- grad_out: float32 [1024, 2048], P('tensor')
- grad_attn_gain: float32 [2048], replicated
- grad_ffn_gain: float32 [2048], replicated
- grad_gate: float32 [2048, 5120], P(None, 'tensor')
- grad_up: float32 [2048, 5120], P(None, 'tensor')
- grad_down: float32 [5120, 2048], P('tensor')
Inputs may be any that keep to these rules, and one draw needn't show every extreme that they name: The first token of every sequence is valid. One sequence has prefix length exactly 512 and another exactly 102.
All inputs are finite; a program needn't handle non-finite values.
Results may differ from a plain program's by a relative error of at most 0.015.
Values may be sent and summed in bfloat16 or wider, within the bound.
A program may use at most 256 MiB of HBM per device.

v0:
```python
import jax
import jax.numpy as jnp
from jax import lax
from jax.sharding import PartitionSpec as P

QUERY_HEADS = 16
KEY_VALUE_HEADS = 4
HEAD_SIZE = 64
SEQ_LEN = 1024
EPSILON = 1e-06


def rope_tables(sequence_length, head_size):
    half_size = head_size // 2
    frequency = 10000.0 ** (-2.0 * jnp.arange(half_size, dtype=jnp.float32) / head_size)
    angles = jnp.arange(sequence_length, dtype=jnp.float32)[:, None] * frequency[None, :]
    cosine = jnp.concatenate([jnp.cos(angles), jnp.cos(angles)], 1)
    sine_tab = jnp.concatenate([jnp.sin(angles), jnp.sin(angles)], 1)
    return (cosine, sine_tab)


def rotate(vector, cosine, sine_tab):
    half_size = vector.shape[-1] // 2
    turned = jnp.concatenate([-vector[..., half_size:], vector[..., :half_size]], -1)
    return vector * cosine + turned * sine_tab


def unrotate(gradient, cosine, sine_tab):
    half_size = gradient.shape[-1] // 2
    shifted = gradient * sine_tab
    return gradient * cosine + jnp.concatenate(
        [shifted[..., half_size:], -shifted[..., :half_size]], -1
    )


def inv_root(vector):
    return lax.rsqrt(jnp.mean(vector * vector, axis=-1, keepdims=True) + EPSILON)


def norm_back(gradient, source, factor, gain_vec):
    scaled = gradient * gain_vec
    return factor * scaled - source * factor**3 * jnp.mean(scaled * source, axis=-1, keepdims=True)


def visible(sequence_length, prefix_len):
    row_pos = jnp.arange(sequence_length)[:, None]
    col_pos = jnp.arange(sequence_length)[None, :]
    return (col_pos <= row_pos) | (row_pos < prefix_len) & (col_pos < prefix_len)


def attend(query_matrix, key_matrix, value_matrix, prefix_len, kv_dev):
    sequence_length, head_count, head_size = query_matrix.shape
    grouped_heads = query_matrix.reshape(sequence_length, kv_dev, head_count // kv_dev, head_size)
    scores = jnp.einsum(
        "ikgd,jkd->kgij", grouped_heads, key_matrix, preferred_element_type=jnp.float32
    ) * head_size ** (-0.5)
    allowed = visible(sequence_length, prefix_len)
    scores = jnp.where(allowed, scores, -1e30)
    row_max = jnp.max(scores, -1, keepdims=True)
    weights = jnp.where(allowed, jnp.exp(scores - row_max), 0.0)
    row_total = jnp.sum(weights, -1, keepdims=True)
    attn_probs = (weights / row_total).astype(jnp.bfloat16)
    attended = jnp.einsum(
        "kgij,jkd->ikgd", attn_probs, value_matrix, preferred_element_type=jnp.float32
    )
    return (
        attended.reshape(sequence_length, head_count * head_size),
        (row_max + jnp.log(row_total))[..., 0],
    )


def attend_back(query_matrix, key_matrix, value_matrix, prefix_len, summit, grad_attended, kv_dev):
    sequence_length, head_count, head_size = query_matrix.shape
    per_group = head_count // kv_dev
    score_scale = head_size ** (-0.5)
    grouped_heads = query_matrix.reshape(sequence_length, kv_dev, per_group, head_size)
    scores = (
        jnp.einsum("ikgd,jkd->kgij", grouped_heads, key_matrix, preferred_element_type=jnp.float32)
        * score_scale
    )
    allowed = visible(sequence_length, prefix_len)
    attn_probs = jnp.where(
        allowed, jnp.exp(jnp.where(allowed, scores, -1e30) - summit[..., None]), 0.0
    )
    grad_heads = grad_attended.reshape(sequence_length, kv_dev, per_group, head_size)
    grad_probs = jnp.einsum(
        "ikgd,jkd->kgij", grad_heads, value_matrix, preferred_element_type=jnp.float32
    )
    inner_sum = jnp.sum(attn_probs * grad_probs, -1, keepdims=True)
    grad_scores = (attn_probs * (grad_probs - inner_sum)).astype(jnp.bfloat16)
    grad_query = (
        jnp.einsum("kgij,jkd->ikgd", grad_scores, key_matrix, preferred_element_type=jnp.float32)
        * score_scale
    )
    grad_key = (
        jnp.einsum("kgij,ikgd->jkd", grad_scores, grouped_heads, preferred_element_type=jnp.float32)
        * score_scale
    )
    grad_value = jnp.einsum(
        "kgij,ikgd->jkd",
        attn_probs.astype(jnp.bfloat16),
        grad_heads,
        preferred_element_type=jnp.float32,
    )
    return (grad_query.reshape(sequence_length, head_count, head_size), grad_key, grad_value)


def body(
    tokens,
    teacher,
    valid,
    prefix,
    w_query,
    key_weight,
    value_weight,
    query_gain,
    key_gain,
    w_out,
    attn_gain,
    ffn_gain,
    w_gate,
    w_up,
    w_down,
):
    rows_dev, width = tokens.shape
    seq_count = prefix.shape[0]
    sequence_length = SEQ_LEN
    group_rows = seq_count * sequence_length
    heads_dev = w_query.shape[1] // HEAD_SIZE
    queries_per_group = QUERY_HEADS // KEY_VALUE_HEADS
    kv_dev = max(1, heads_dev // queries_per_group)
    query_cols = heads_dev * HEAD_SIZE
    kv_cols = kv_dev * HEAD_SIZE
    kv_start = lax.axis_index("tensor") * heads_dev // queries_per_group * HEAD_SIZE
    key_local = lax.dynamic_slice_in_dim(key_weight, kv_start, kv_cols, 1)
    value_local = lax.dynamic_slice_in_dim(value_weight, kv_start, kv_cols, 1)
    source = tokens.astype(jnp.float32)
    factor_one = inv_root(source)
    normed_input = (source * factor_one * attn_gain).astype(jnp.bfloat16)
    normed_all = lax.all_gather(normed_input, "tensor", axis=0, tiled=True)
    proj_weight = jnp.concatenate([w_query, key_local, value_local], 1)
    projected = jnp.dot(normed_all, proj_weight, preferred_element_type=jnp.float32)
    query_raw = projected[:, :query_cols].reshape(group_rows, heads_dev, HEAD_SIZE)
    key_raw = projected[:, query_cols : query_cols + kv_cols].reshape(group_rows, kv_dev, HEAD_SIZE)
    value_low = (
        projected[:, query_cols + kv_cols :]
        .astype(jnp.bfloat16)
        .reshape(seq_count, sequence_length, kv_dev, HEAD_SIZE)
    )
    query_factor = inv_root(query_raw)
    key_factor = inv_root(key_raw)
    cosine, sine_tab = rope_tables(sequence_length, HEAD_SIZE)
    cos_rows = jnp.tile(cosine, (seq_count, 1))[:, None, :]
    sin_rows = jnp.tile(sine_tab, (seq_count, 1))[:, None, :]
    query_low = (
        rotate(query_raw * query_factor * query_gain, cos_rows, sin_rows)
        .astype(jnp.bfloat16)
        .reshape(seq_count, sequence_length, heads_dev, HEAD_SIZE)
    )
    key_low = (
        rotate(key_raw * key_factor * key_gain, cos_rows, sin_rows)
        .astype(jnp.bfloat16)
        .reshape(seq_count, sequence_length, kv_dev, HEAD_SIZE)
    )
    attended, summit = lax.map(
        lambda packed: attend(packed[0], packed[1], packed[2], packed[3], kv_dev),
        (query_low, key_low, value_low, prefix),
    )
    attended_low = attended.reshape(group_rows, query_cols).astype(jnp.bfloat16)
    middle = source + lax.psum_scatter(
        jnp.dot(attended_low, w_out, preferred_element_type=jnp.float32),
        "tensor",
        scatter_dimension=0,
        tiled=True,
    )
    factor_two = inv_root(middle)
    normed_two = (middle * factor_two * ffn_gain).astype(jnp.bfloat16)
    normed_two_all = lax.all_gather(normed_two, "tensor", axis=0, tiled=True)
    gate_act = jnp.dot(normed_two_all, w_gate, preferred_element_type=jnp.float32)
    up_act = jnp.dot(normed_two_all, w_up, preferred_element_type=jnp.float32)
    sig_gate = jax.nn.sigmoid(gate_act)
    hidden = (gate_act * sig_gate * up_act).astype(jnp.bfloat16)
    result = middle + lax.psum_scatter(
        jnp.dot(hidden, w_down, preferred_element_type=jnp.float32).astype(jnp.bfloat16),
        "tensor",
        scatter_dimension=0,
        tiled=True,
    ).astype(jnp.float32)
    mask_rows = valid.astype(jnp.float32)[:, None]
    error_rows = result - teacher.astype(jnp.float32)
    total_count, total_square = lax.psum(
        (jnp.sum(valid).astype(jnp.float32), jnp.sum(error_rows * error_rows * mask_rows)),
        ("dp", "tensor"),
    )
    loss = total_square / (total_count * width)
    cotangent = group_rows * lax.axis_size("dp") / total_count * error_rows * mask_rows
    cot_all = lax.all_gather(cotangent.astype(jnp.bfloat16), "tensor", axis=0, tiled=True)
    grad_down = jnp.einsum("tf,td->fd", hidden, cot_all, preferred_element_type=jnp.float32)
    grad_hidden = jnp.einsum("td,fd->tf", cot_all, w_down, preferred_element_type=jnp.float32)
    grad_gate_low = (grad_hidden * up_act * sig_gate * (1.0 + gate_act * (1.0 - sig_gate))).astype(
        jnp.bfloat16
    )
    grad_up_low = (grad_hidden * gate_act * sig_gate).astype(jnp.bfloat16)
    gate_part = grad_gate_low
    up_part = grad_up_low
    grad_normed_two = lax.psum_scatter(
        (
            jnp.einsum("tf,df->td", gate_part, w_gate, preferred_element_type=jnp.float32)
            + jnp.einsum("tf,df->td", up_part, w_up, preferred_element_type=jnp.float32)
        ).astype(jnp.bfloat16),
        "tensor",
        scatter_dimension=0,
        tiled=True,
    ).astype(jnp.float32)
    grad_ffn_gain = jnp.sum(grad_normed_two * middle * factor_two, 0)
    grad_middle = cotangent + norm_back(grad_normed_two, middle, factor_two, ffn_gain)
    grad_branch_all = lax.all_gather(grad_middle.astype(jnp.bfloat16), "tensor", axis=0, tiled=True)
    grad_out = jnp.einsum(
        "tq,td->qd", attended_low, grad_branch_all, preferred_element_type=jnp.float32
    )
    grad_attended = jnp.einsum(
        "td,qd->tq", grad_branch_all, w_out, preferred_element_type=jnp.float32
    ).astype(jnp.bfloat16)
    grad_q_rot, grad_k_rot, grad_v = lax.map(
        lambda packed: attend_back(
            packed[0], packed[1], packed[2], packed[3], packed[4], packed[5], kv_dev
        ),
        (
            query_low,
            key_low,
            value_low,
            prefix,
            summit,
            grad_attended.reshape(seq_count, sequence_length, query_cols),
        ),
    )
    grad_k_rot = grad_k_rot.reshape(group_rows, kv_dev, HEAD_SIZE)
    grad_v = grad_v.reshape(group_rows, kv_cols)
    grad_q_normed = unrotate(
        grad_q_rot.reshape(group_rows, heads_dev, HEAD_SIZE), cos_rows, sin_rows
    )
    grad_k_normed = unrotate(grad_k_rot, cos_rows, sin_rows)
    grad_query_gain = jnp.sum(grad_q_normed * query_raw * query_factor, (0, 1))
    grad_key_gain = jnp.sum(grad_k_normed * key_raw * key_factor, (0, 1))
    grad_q_raw = norm_back(grad_q_normed, query_raw, query_factor, query_gain)
    grad_k_raw = norm_back(grad_k_normed, key_raw, key_factor, key_gain)
    back_rows = jnp.concatenate(
        [
            grad_q_raw.reshape(group_rows, query_cols),
            grad_k_raw.reshape(group_rows, kv_cols),
            grad_v,
        ],
        1,
    ).astype(jnp.bfloat16)
    grad_normed = lax.psum_scatter(
        jnp.einsum("tc,dc->td", back_rows, proj_weight, preferred_element_type=jnp.float32).astype(
            jnp.bfloat16
        ),
        "tensor",
        scatter_dimension=0,
        tiled=True,
    ).astype(jnp.float32)
    grad_attn_gain = jnp.sum(grad_normed * source * factor_one, 0)
    grad_tokens = grad_middle + norm_back(grad_normed, source, factor_one, attn_gain)
    grad_proj = jnp.einsum(
        "td,tc->dc",
        lax.all_gather(normed_input, "tensor", axis=0, tiled=True),
        back_rows,
        preferred_element_type=jnp.float32,
    )
    shard_rows = lax.all_gather(normed_two, "tensor", axis=0, tiled=True)
    gate_part = grad_gate_low
    up_part = grad_up_low
    grad_gate = jnp.einsum("td,tf->df", shard_rows, gate_part, preferred_element_type=jnp.float32)
    grad_up = jnp.einsum("td,tf->df", shard_rows, up_part, preferred_element_type=jnp.float32)
    grad_query = grad_proj[:, :query_cols]
    zero_kv = jnp.zeros((width, key_weight.shape[1]), jnp.float32)
    key_full = lax.dynamic_update_slice_in_dim(
        zero_kv, grad_proj[:, query_cols : query_cols + kv_cols], kv_start, 1
    )
    value_full = lax.dynamic_update_slice_in_dim(
        zero_kv, grad_proj[:, query_cols + kv_cols :], kv_start, 1
    )
    grad_query, grad_out, grad_gate, grad_up, grad_down = (
        lax.psum(grad_query.astype(jnp.bfloat16), "dp").astype(jnp.float32),
        lax.psum(grad_out.astype(jnp.bfloat16), "dp").astype(jnp.float32),
        lax.psum(grad_gate.astype(jnp.bfloat16), "dp").astype(jnp.float32),
        lax.psum(grad_up.astype(jnp.bfloat16), "dp").astype(jnp.float32),
        lax.psum(grad_down.astype(jnp.bfloat16), "dp").astype(jnp.float32),
    )
    key_full, value_full, grad_query_gain, grad_key_gain, grad_attn_gain, grad_ffn_gain = lax.psum(
        (key_full, value_full, grad_query_gain, grad_key_gain, grad_attn_gain, grad_ffn_gain),
        ("dp", "tensor"),
    )
    return (
        result.astype(jnp.bfloat16),
        loss,
        grad_tokens,
        grad_query,
        key_full,
        value_full,
        grad_query_gain,
        grad_key_gain,
        grad_out,
        grad_attn_gain,
        grad_ffn_gain,
        grad_gate,
        grad_up,
        grad_down,
    )


def solution(mesh):
    placed = (
        P(("dp", "tensor"), None),
        P(("dp", "tensor"), None),
        P(("dp", "tensor")),
        P("dp"),
        P(None, "tensor"),
        P(),
        P(),
        P(),
        P(),
        P("tensor", None),
        P(),
        P(),
        P(None, "tensor"),
        P(None, "tensor"),
        P("tensor", None),
    )
    return jax.shard_map(
        body,
        mesh=mesh,
        in_specs=placed,
        out_specs=(
            P(("dp", "tensor"), None),
            P(),
            P(("dp", "tensor"), None),
            P(None, "tensor"),
            P(),
            P(),
            P(),
            P(),
            P("tensor", None),
            P(),
            P(),
            P(None, "tensor"),
            P(None, "tensor"),
            P("tensor", None),
        ),
        check_vma=False,
    )
```

profile of v0, /device:TPU:0, one launch (start us, length us, event | category | flops | bytes accessed | tf_op | source)
XLA Modules:
  0.0 2096.8 jit_solution(9297197625935668544)
XLA Ops:
  17.7 148.8 %all-gather.5.cloned.1.call-done = bf16[2048,2048]{1,0:T(8,128)(2,1)} async-done(((bf16[512,2048]{1,0:T(8,128)(2,1)}), bf16[2048,2048]{1,0:T(8,128)(2,1)}) %all-gather.5.cloned.1.call-update) | async-done | bytes 8388624 | tf_op jit(solution)/shard_map/all_gather | solution.py:140
  196.8 34.9 %while.26 = (s32[]{:T(128)}, bf16[2,1024,256]{2,1,0:T(8,128)(2,1)}, f32[2,1,4,1024]{3,2,1,0:T(4,128)}, bf16[2,1024,1,64]{1,3,2,0:T(8,128)(2,1)S(1)}, s32[2]{0:T(...) while((s32[]{:T(128)}, bf16[2,1024,256]{2,1,0:T(8,128)(2,1)}, ...), condition=%wide.region_6.7_spmd, body=%wide.region_3.6_spmd.sunk | while | flops 1135604736 | bytes 58068088 | solution.py:165
  241.6 278.6 %reduce-scatter.5.cloned.1.call-done = f32[512,2048]{1,0:T(8,128)} async-done(((f32[2048,2048]{1,0:T(8,128)}), f32[512,2048]{1,0:T(8,128)}) %reduce-scatter.5.cloned.1.call-update) | async-done | bytes 4194320 | tf_op jit(solution)/shard_map/reduce_scatter | solution.py:170
  530.1 150.5 %all-gather.7.cloned.1.call-done = bf16[2048,2048]{1,0:T(8,128)(2,1)} async-done(((bf16[512,2048]{1,0:T(8,128)(2,1)}), bf16[2048,2048]{1,0:T(8,128)(2,1)}) %all-gather.7.cloned.1.call-update) | async-done | bytes 8388624 | tf_op jit(solution)/shard_map/all_gather | solution.py:178
  680.6 16.8 fusion.94
  697.5 17.2 multiply_convert_fusion.2
  714.7 16.6 convolution_convert_fusion.1
  733.2 43.1 %psum.92 = f32[]{:T(128)} all-reduce(f32[]{:T(128)S(6)} %convert_element_type.123), channel_id=1, replica_groups=mesh['dp'=8,'tensor'=4] {'dp','tensor'}, use_global_device_ids=true, to_apply=%region_13.14 | all-reduce | flops 1 | bytes 8 | tf_op jit(solution)/shard_map/psum | solution.py:191
  777.0 98.1 %reduce-scatter.7.cloned.1.call-done = bf16[512,2048]{1,0:T(8,128)(2,1)} async-done(((bf16[2048,2048]{1,0:T(8,128)(2,1)}), bf16[512,2048]{1,0:T(8,128)(2,1)}) %reduce-scatter.7.cloned.1.call-update) | async-done | bytes 2097168 | tf_op jit(solution)/shard_map/reduce_scatter | solution.py:183
  880.6 150.5 %all-gather.9.cloned.1.call-done = bf16[2048,2048]{1,0:T(8,128)(2,1)} async-done(((bf16[512,2048]{1,0:T(8,128)(2,1)}), bf16[2048,2048]{1,0:T(8,128)(2,1)}) %all-gather.9.cloned.1.call-update) | async-done | bytes 8388624 | tf_op jit(solution)/shard_map/all_gather | solution.py:197
  1031.1 24.3 %multiply_convert_fusion = (bf16[2048,1280]{1,0:T(8,128)(2,1)}, bf16[2048,1280]{1,0:T(8,128)(2,1)}) fusion(f32[2048,1280]{1,0:T(8,128)} %fusion.94, f32[2048,1280]{1,0:T(8,128)} %get-tuple-element.296, bf16[2048,2048]{1,0:T(8,128)(2,1)} %all-gather.9.cloned.1.call-done, bf16[1280,2048]{1,0:T(8,128)(2,1)} %param.33), kind=kOutput, calls=%fused_computation.65 | convolution fusion | flops 10771496960 | bytes 45088768 | tf_op jit(solution)/shard_map/td,fd->tf/dot_general | solution.py:199
  1055.4 17.9 fusion.95
  1073.3 19.4 add_convert_fusion
  1092.8 142.8 %reduce-scatter.9.cloned.1.call-done = bf16[512,2048]{1,0:T(8,128)(2,1)} async-done(((bf16[2048,2048]{1,0:T(8,128)(2,1)}), bf16[512,2048]{1,0:T(8,128)(2,1)}) %reduce-scatter.9.cloned.1.call-update) | async-done | bytes 2097168 | tf_op jit(solution)/shard_map/reduce_scatter | solution.py:206
  1250.9 16.9 convolution_convert_fusion.2
  1267.8 15.5 convolution_convert_fusion.3
  1297.1 101.2 %all-gather.11.cloned.1.call-done = bf16[2048,2048]{1,0:T(8,128)(2,1)} async-done(((bf16[512,2048]{1,0:T(8,128)(2,1)}), bf16[2048,2048]{1,0:T(8,128)(2,1)}) %all-gather.11.cloned.1.call-update) | async-done | bytes 8388624 | tf_op jit(solution)/shard_map/all_gather | solution.py:217
  1405.0 125.9 %while.27 = (s32[]{:T(128)}, f32[2,1024,4,64]{1,0,3,2:T(2,128)}, f32[2,1024,1,64]{1,0,3,2:T(2,128)}, bf16[2,1024,1,64]{1,3,2,0:T(8,128)(2,1)}, bf16[2,1024,1,64]...) while((s32[]{:T(128)}, f32[2,1024,4,64]{1,0,3,2:T(2,128)}, ...), condition=%wide.region_18.19_spmd, body=%wide.region_16.18_spmd.sunk | while | flops 2729767936 | bytes 147803392 | solution.py:224
  1449.3 18.9 dynamic_update_slice.38
  1511.9 18.9 dynamic_update_slice.38
  1590.0 197.7 %all-reduce.8.cloned.1.call-done = (bf16[2048,256]{0,1:T(8,128)(2,1)}, bf16[256,2048]{1,0:T(8,128)(2,1)}, bf16[2048,1280]{1,0:T(8,128)(2,1)}, bf16[2048,1280]{1,0:T(8,128)(2,1)}, bf16[1280,2048]{1,0:T(8,128)(2,1)}) async-done(((bf16[2048,256]{0,1:T(8,128)(2,1)}, bf16[256,2048]{1,0:T(8,128)(2,1)}, bf16[2048,1280]{1,0:T(8,128)(2,1)}, bf16[2048,1280]{1,0:T(8,128)(2,1)}, bf16[1280,2048]{1,0:T(8,128)(2,1)}), ...) | async-done | bytes 17825808 | tf_op jit(solution)/shard_map/psum | solution.py:285
  1811.2 123.4 %reduce-scatter.11.cloned.1.call-done = bf16[512,2048]{1,0:T(8,128)(2,1)} async-done(((bf16[2048,2048]{1,0:T(8,128)(2,1)}), bf16[512,2048]{1,0:T(8,128)(2,1)}) %reduce-scatter.11.cloned.1.call-update) | async-done | bytes 2097168 | tf_op jit(solution)/shard_map/reduce_scatter | solution.py:255
  1937.8 41.8 %all-reduce = (f32[]{:T(128)}, f32[64]{0:T(128)}, f32[64]{0:T(128)}, f32[2048]{0:T(1024)}, f32[2048]{0:T(1024)}) all-reduce(f32[]{:T(128)} %get-tuple-element.206, f32[64]{0:T(128)S(1)} %reduce_sum.163, f32[64]{0:T(128)S(1)} %get-tuple-element.209, ...), channel_id=1, replica_groups=mesh['dp'=8,'tensor'=4] {'dp','tensor'}, use_global_device_ids=true, to_apply=%region_11.12 | all-reduce | flops 4225 | bytes 33800 | tf_op jit(solution)/shard_map/psum | solution.py:191
  1986.4 97.6 %all-reduce.6.cloned.1.call-done = (f32[2048,256]{1,0:T(8,128)}, f32[2048,256]{1,0:T(8,128)}) async-done(((f32[2048,256]{1,0:T(8,128)}, f32[2048,256]{1,0:T(8,128)}), (f32[2048,256]{1,0:T(8,128)}, f32[2048,256]{1,0:T(8,128)})) %all-reduce.6.cloned.1.call-update) | async-done | bytes 4194320 | tf_op jit(solution)/shard_map/psum | solution.py:291
  (315 shorter events, 319.8 us)
Async XLA Ops:
  7.2 224.5 %copy-start = (bf16[256,2048]{1,0:T(8,128)(2,1)S(1)}, bf16[256,2048]{1,0:T(8,128)(2,1)}, u32[]{:S(2)}) copy-start(bf16[256,2048]{1,0:T(8,128)(2,1)} %param.28) | copy-start | bytes 3145732
  7.2 159.3 %all-gather.5.cloned.1.call-start = ((), (), s32[]{:S(2)}) async-start(), calls=%async_computation.4 | async-start | bytes 10485760 | tf_op jit(solution)/shard_map/all_gather | solution.py:140
  14.0 506.2 %reduce-scatter.5.cloned.1.call-start = ((), (), s32[]{:S(2)}) async-start(), calls=%async_computation.5 | async-start | bytes 20971520 | tf_op jit(solution)/shard_map/reduce_scatter | solution.py:170
  15.1 163.1 %copy-start.16 = (f32[8,8,2,1024]{3,1,2,0:T(8,128)}, f32[8,8,2,1024]{3,1,2,0:T(8,128)S(1)}, u32[]{:S(2)}) copy-start(f32[8,8,2,1024]{3,1,2,0:T(8,128)S(1)} %copy.112) | copy-start | bytes 1572868
  15.9 162.3 %copy-start.7 = (f32[8,8,2,1024]{3,1,2,0:T(8,128)}, f32[8,8,2,1024]{3,1,2,0:T(8,128)S(1)}, u32[]{:S(2)}) copy-start(f32[8,8,2,1024]{3,1,2,0:T(8,128)S(1)} %copy.111) | copy-start | bytes 1572868
  17.7 156.1 %copy-start.28 = (bf16[2048,64]{1,0:T(8,128)(2,1)}, bf16[2048,64]{1,0:T(8,128)(2,1)S(1)}, u32[]{:S(2)}) copy-start(bf16[2048,64]{1,0:T(8,128)(2,1)S(1)} %get-tuple-element.297) | copy-start | bytes 786436
  17.7 156.1 %copy-start.30 = (bf16[2048,64]{1,0:T(8,128)(2,1)}, bf16[2048,64]{1,0:T(8,128)(2,1)S(1)}, u32[]{:S(2)}) copy-start(bf16[2048,64]{1,0:T(8,128)(2,1)S(1)} %get-tuple-element.298) | copy-start | bytes 786436
  241.5 278.7 %copy-start.3 = (bf16[512,2048]{1,0:T(8,128)(2,1)S(1)}, bf16[512,2048]{1,0:T(8,128)(2,1)}, u32[]{:S(2)}) copy-start(bf16[512,2048]{1,0:T(8,128)(2,1)} %param.19) | copy-start | bytes 6291460
  241.6 284.6 %copy-start.36 = (f32[2048]{0:T(1024)S(1)}, f32[2048]{0:T(1024)}, u32[]{:S(2)}) copy-start(f32[2048]{0:T(1024)} %param.30) | copy-start | bytes 24580
  241.6 439.1 %all-gather.7.cloned.1.call-start = ((), (), s32[]{:S(2)}) async-start(), calls=%async_computation.6 | async-start | bytes 10485760 | tf_op jit(solution)/shard_map/all_gather | solution.py:178
  530.1 345.0 %reduce-scatter.7.cloned.1.call-start = ((), (), s32[]{:S(2)}) async-start(), calls=%async_computation.7 | async-start | bytes 10485760 | tf_op jit(solution)/shard_map/reduce_scatter | solution.py:183
  731.2 143.9 %copy-start.5 = (bf16[512,2048]{1,0:T(8,128)(2,1)S(1)}, bf16[512,2048]{1,0:T(8,128)(2,1)}, u32[]{:S(2)}) copy-start(bf16[512,2048]{1,0:T(8,128)(2,1)} %param.20) | copy-start | bytes 6291460
  731.3 299.8 %all-gather.9.cloned.1.call-start = ((), (), s32[]{:S(2)}) async-start(), calls=%async_computation.8 | async-start | bytes 10485760 | tf_op jit(solution)/shard_map/all_gather | solution.py:197
  880.6 355.0 %reduce-scatter.9.cloned.1.call-start = ((), (), s32[]{:S(2)}) async-start(), calls=%async_computation.9 | async-start | bytes 10485760 | tf_op jit(solution)/shard_map/reduce_scatter | solution.py:206
  1092.7 142.9 %copy-start.37 = (f32[2048]{0:T(1024)S(1)}, f32[2048]{0:T(1024)}, u32[]{:S(2)}) copy-start(f32[2048]{0:T(1024)} %param.30) | copy-start | bytes 24580
  1092.7 142.9 %copy-start.44 = (f32[512]{0:T(512)S(1)}, f32[512]{0:T(512)}, u32[]{:S(2)}) copy-start(f32[512]{0:T(512)} %copy-done.43) | copy-start | bytes 6148
  1092.7 148.7 %copy-start.48 = (f32[512]{0:T(512)S(1)}, f32[512]{0:T(512)}, u32[]{:S(2)}) copy-start(f32[512]{0:T(512)} %get-tuple-element.289) | copy-start | bytes 6148
  1092.7 305.6 %all-gather.11.cloned.1.call-start = ((), (), s32[]{:S(2)}) async-start(), calls=%async_computation.10 | async-start | bytes 10485760 | tf_op jit(solution)/shard_map/all_gather | solution.py:217
  1247.8 540.0 %all-reduce.8.cloned.1.call-start = ((), (), s32[]{:S(2)}) async-start(), calls=%async_computation.13 | async-start | bytes 35651584 | tf_op jit(solution)/shard_map/psum | solution.py:285
  1558.4 376.3 %reduce-scatter.11.cloned.1.call-start = ((), (), s32[]{:S(2)}) async-start(), calls=%async_computation.11 | async-start | bytes 10485760 | tf_op jit(solution)/shard_map/reduce_scatter | solution.py:255
  1568.8 515.2 %all-reduce.6.cloned.1.call-start = ((), (), s32[]{:S(2)}) async-start(), calls=%async_computation.12 | async-start | bytes 8388608 | tf_op jit(solution)/shard_map/psum | solution.py:291
  1805.7 128.9 %copy-start.4 = (bf16[512,2048]{1,0:T(8,128)(2,1)S(1)}, bf16[512,2048]{1,0:T(8,128)(2,1)}, u32[]{:S(2)}) copy-start(bf16[512,2048]{1,0:T(8,128)(2,1)} %param.19) | copy-start | bytes 6291460
  1805.7 128.9 %copy-start.38 = (f32[2048]{0:T(1024)S(1)}, f32[2048]{0:T(1024)}, u32[]{:S(2)}) copy-start(f32[2048]{0:T(1024)} %param.29) | copy-start | bytes 24580
  1811.2 169.1 %copy-start.51 = (f32[512]{0:T(512)S(1)}, f32[512]{0:T(512)}, u32[]{:S(2)}) copy-start(f32[512]{0:T(512)} %get-tuple-element.287) | copy-start | bytes 6148
  (61 other events, 759.7 us)
Sparse Core Ops, SparseCore 0:
  14.1 152.3 all-gather.4
  241.7 278.5 reduce-scatter.4
  530.2 150.3 all-gather.6
  731.4 143.6 reduce-scatter.6
  880.7 150.3 all-gather.8
  1092.8 142.6 reduce-scatter.8
  1247.9 150.3 all-gather.10
  1558.5 229.2 all-reduce.7
  1790.1 144.4 reduce-scatter.10
  1940.8 143.1 all-reduce.5
where the time goes:
time: 2110 us; the launch traced here: 2100 us
  waiting for transfers between devices  1490 us (71%)
  matrix products  273 us (13%)
  local copies, waits for them, and re-layouts  115 us (5%)
  other arithmetic  113 us (5%)
  blocking collectives  84.9 us (4%)
    reduce_scatter x1, waiting for transfers between devices, body(): lax.psum_scatter(jnp.dot(attended_low, w_out, preferred_element_type=jnp....  279 us
    psum x1, waiting for transfers between devices, body(): lax.psum(grad_query.astype(jnp.bfloat16), 'dp').astype(jnp.float32)  198 us
    all_gather x1, waiting for transfers between devices, body(): normed_two_all = lax.all_gather(normed_two, 'tensor', axis=0, tiled=True)  150 us
    all_gather x1, waiting for transfers between devices, body(): lax.all_gather(cotangent.astype(jnp.bfloat16), 'tensor', axis=0, tiled=True)  150 us
    all_gather x1, waiting for transfers between devices, body(): normed_all = lax.all_gather(normed_input, 'tensor', axis=0, tiled=True)  149 us
    reduce_scatter x1, waiting for transfers between devices, body(): lax.psum_scatter((jnp.einsum('tf,df->td', gate_part, w_gate, preferred_el...  143 us
    reduce_scatter x1, waiting for transfers between devices, body(): lax.psum_scatter(jnp.einsum('tc,dc->td', back_rows, proj_weight, preferre...  123 us
    all_gather x1, waiting for transfers between devices, body(): lax.all_gather(grad_middle.astype(jnp.bfloat16), 'tensor', axis=0, tiled=...  101 us
  transfers between devices with their start and end apart: 10, of which 10 were waited for; matrix products, arithmetic and copies ran while one was open for 5% of the time, Pallas kernels for 0%

commit v1 on v0

--- a/solution.py
+++ b/solution.py
@@ -282,7 +282,7 @@
         zero_kv, grad_proj[:, query_cols + kv_cols :], kv_start, 1
     )
     grad_query, grad_out, grad_gate, grad_up, grad_down = (
-        lax.psum(grad_query.astype(jnp.bfloat16), "dp").astype(jnp.float32),
+        jnp.sum(lax.all_gather(grad_query.astype(jnp.bfloat16), "dp"), axis=0).astype(jnp.float32),
         lax.psum(grad_out.astype(jnp.bfloat16), "dp").astype(jnp.float32),
         lax.psum(grad_gate.astype(jnp.bfloat16), "dp").astype(jnp.float32),
         lax.psum(grad_up.astype(jnp.bfloat16), "dp").astype(jnp.float32),

time: 2110 us -> 2000 us (0.948)
  waiting for transfers between devices: 1490 us -> 1350 us
    psum x1, waiting for transfers between devices: 198 us -> 26.6 us  [body(): lax.psum(grad_out.astype(jnp.bfloat16), 'dp').astype(jnp.float32)]
    all_gather x0 -> x1, waiting for transfers between devices: none -> 35.9 us  [body(): lax.all_gather(grad_query.astype(jnp.bfloat16), 'dp')]
  transfers between devices with their start and end apart: 10 -> 11, of which waited for: 10 -> 11; matrix products, arithmetic and copies ran while one was open for 5% -> 15% of each run, Pallas kernels for 0% -> 0%
where the time goes in v1:
time: 2000 us; the launch traced here: 1990 us
  waiting for transfers between devices  1350 us (68%)
  matrix products  279 us (14%)
  local copies, waits for them, and re-layouts  136 us (7%)
  other arithmetic  121 us (6%)
  blocking collectives  85 us (4%)
    reduce_scatter x1, waiting for transfers between devices, body(): lax.psum_scatter(jnp.dot(attended_low, w_out, preferred_element_type=jnp....  279 us
    all_gather x1, waiting for transfers between devices, body(): normed_two_all = lax.all_gather(normed_two, 'tensor', axis=0, tiled=True)  150 us
    all_gather x1, waiting for transfers between devices, body(): lax.all_gather(cotangent.astype(jnp.bfloat16), 'tensor', axis=0, tiled=True)  150 us
    all_gather x1, waiting for transfers between devices, body(): normed_all = lax.all_gather(normed_input, 'tensor', axis=0, tiled=True)  149 us
    reduce_scatter x1, waiting for transfers between devices, body(): lax.psum_scatter((jnp.einsum('tf,df->td', gate_part, w_gate, preferred_el...  143 us
    reduce_scatter x1, waiting for transfers between devices, body(): lax.psum_scatter(jnp.einsum('tc,dc->td', back_rows, proj_weight, preferre...  116 us
    all_gather x1, waiting for transfers between devices, body(): lax.all_gather(grad_middle.astype(jnp.bfloat16), 'tensor', axis=0, tiled=...  101 us
    reduce_scatter x1, waiting for transfers between devices, body(): lax.psum_scatter(jnp.dot(hidden, w_down, preferred_element_type=jnp.float...  98.1 us
  transfers between devices with their start and end apart: 11, of which 11 were waited for; matrix products, arithmetic and copies ran while one was open for 15% of the time, Pallas kernels for 0%

profile of v1, /device:TPU:0, one launch (start us, length us, event | category | flops | bytes accessed | tf_op | source)
XLA Modules:
  0.0 1988.1 jit_solution(3349286924488627420)
XLA Ops:
  17.7 148.8 %all-gather.7.cloned.1.call-done = bf16[2048,2048]{1,0:T(8,128)(2,1)} async-done(((bf16[512,2048]{1,0:T(8,128)(2,1)}), bf16[2048,2048]{1,0:T(8,128)(2,1)}) %all-gather.7.cloned.1.call-update) | async-done | bytes 8388624 | tf_op jit(solution)/shard_map/all_gather | solution.py:140
  196.8 34.9 %while.26 = (s32[]{:T(128)}, bf16[2,1024,256]{2,1,0:T(8,128)(2,1)}, f32[2,1,4,1024]{3,2,1,0:T(4,128)}, bf16[2,1024,1,64]{1,3,2,0:T(8,128)(2,1)S(1)}, s32[2]{0:T(...) while((s32[]{:T(128)}, bf16[2,1024,256]{2,1,0:T(8,128)(2,1)}, ...), condition=%wide.region_6.7_spmd, body=%wide.region_3.6_spmd.sunk | while | flops 1135604736 | bytes 58068088 | solution.py:165
  241.6 278.6 %reduce-scatter.5.cloned.1.call-done = f32[512,2048]{1,0:T(8,128)} async-done(((f32[2048,2048]{1,0:T(8,128)}), f32[512,2048]{1,0:T(8,128)}) %reduce-scatter.5.cloned.1.call-update) | async-done | bytes 4194320 | tf_op jit(solution)/shard_map/reduce_scatter | solution.py:170
  530.1 150.5 %all-gather.9.cloned.1.call-done = bf16[2048,2048]{1,0:T(8,128)(2,1)} async-done(((bf16[512,2048]{1,0:T(8,128)(2,1)}), bf16[2048,2048]{1,0:T(8,128)(2,1)}) %all-gather.9.cloned.1.call-update) | async-done | bytes 8388624 | tf_op jit(solution)/shard_map/all_gather | solution.py:178
  680.6 16.8 fusion.94
  697.5 17.2 multiply_convert_fusion.2
  714.7 16.6 convolution_convert_fusion.1
  733.2 43.1 %psum.85 = f32[]{:T(128)} all-reduce(f32[]{:T(128)S(6)} %convert_element_type.125), channel_id=1, replica_groups=mesh['dp'=8,'tensor'=4] {'dp','tensor'}, use_global_device_ids=true, to_apply=%region_13.14 | all-reduce | flops 1 | bytes 8 | tf_op jit(solution)/shard_map/psum | solution.py:191
  777.0 98.1 %reduce-scatter.7.cloned.1.call-done = bf16[512,2048]{1,0:T(8,128)(2,1)} async-done(((bf16[2048,2048]{1,0:T(8,128)(2,1)}), bf16[512,2048]{1,0:T(8,128)(2,1)}) %reduce-scatter.7.cloned.1.call-update) | async-done | bytes 2097168 | tf_op jit(solution)/shard_map/reduce_scatter | solution.py:183
  880.6 150.5 %all-gather.11.cloned.1.call-done = bf16[2048,2048]{1,0:T(8,128)(2,1)} async-done(((bf16[512,2048]{1,0:T(8,128)(2,1)}), bf16[2048,2048]{1,0:T(8,128)(2,1)}) %all-gather.11.cloned.1.call-update) | async-done | bytes 8388624 | tf_op jit(solution)/shard_map/all_gather | solution.py:197
  1031.1 24.3 %multiply_convert_fusion = (bf16[2048,1280]{1,0:T(8,128)(2,1)}, bf16[2048,1280]{1,0:T(8,128)(2,1)}) fusion(f32[2048,1280]{1,0:T(8,128)} %fusion.94, f32[2048,1280]{1,0:T(8,128)} %get-tuple-element.298, bf16[2048,2048]{1,0:T(8,128)(2,1)} %all-gather.11.cloned.1.call-done, bf16[1280,2048]{1,0:T(8,128)(2,1)} %param.33), kind=kOutput, calls=%fused_computation.65 | convolution fusion | flops 10771496960 | bytes 45088768 | tf_op jit(solution)/shard_map/td,fd->tf/dot_general | solution.py:199
  1055.3 17.8 fusion.95
  1073.2 19.4 add_convert_fusion
  1092.7 142.8 %reduce-scatter.9.cloned.1.call-done = bf16[512,2048]{1,0:T(8,128)(2,1)} async-done(((bf16[2048,2048]{1,0:T(8,128)(2,1)}), bf16[512,2048]{1,0:T(8,128)(2,1)}) %reduce-scatter.9.cloned.1.call-update) | async-done | bytes 2097168 | tf_op jit(solution)/shard_map/reduce_scatter | solution.py:206
  1250.7 17.0 convolution_convert_fusion.2
  1296.9 101.2 %all-gather.13.cloned.1.call-done = bf16[2048,2048]{1,0:T(8,128)(2,1)} async-done(((bf16[512,2048]{1,0:T(8,128)(2,1)}), bf16[2048,2048]{1,0:T(8,128)(2,1)}) %all-gather.13.cloned.1.call-update) | async-done | bytes 8388624 | tf_op jit(solution)/shard_map/all_gather | solution.py:217
  1411.7 128.2 %while.27 = (s32[]{:T(128)}, f32[2,1024,4,64]{1,0,3,2:T(2,128)}, f32[2,1024,1,64]{1,0,3,2:T(2,128)}, bf16[2,1024,1,64]{1,3,2,0:T(8,128)(2,1)}, bf16[2,1024,1,64]...) while((s32[]{:T(128)}, f32[2,1024,4,64]{1,0,3,2:T(2,128)}, ...), condition=%wide.region_18.19_spmd, body=%wide.region_16.18_spmd.sunk | while | flops 2729767936 | bytes 147803392 | solution.py:224
  1457.4 18.9 dynamic_update_slice.38
  1520.8 18.9 dynamic_update_slice.38
  1596.1 26.6 %all-reduce.8.cloned.1.call-done = (bf16[256,2048]{1,0:T(8,128)(2,1)}, bf16[2048,1280]{1,0:T(8,128)(2,1)}, bf16[2048,1280]{1,0:T(8,128)(2,1)}, bf16[1280,2048]{1,0:T(8,128)(2,1)}) async-done(((bf16[256,2048]{1,0:T(8,128)(2,1)}, bf16[2048,1280]{1,0:T(8,128)(2,1)}, bf16[2048,1280]{1,0:T(8,128)(2,1)}, bf16[1280,2048]{1,0:T(8,128)(2,1)}), (bf16[256,2048]{1,0:T(8,128)(2,1)}, bf16[2048,1280]{1,0:T(8,128)(2,1)}, ...) | async-done | bytes 16777232 | tf_op jit(solution)/shard_map/psum | solution.py:286
  1643.7 35.9 %all-gather.15.cloned.1.call-done = bf16[16384,256]{0,1:T(8,128)(2,1)} async-done(((bf16[2048,256]{0,1:T(8,128)(2,1)}), bf16[16384,256]{0,1:T(8,128)(2,1)}) %all-gather.15.cloned.1.call-update) | async-done | bytes 8388624 | tf_op jit(solution)/shard_map/all_gather | solution.py:285
  1709.8 116.4 %reduce-scatter.11.cloned.1.call-done = bf16[512,2048]{1,0:T(8,128)(2,1)} async-done(((bf16[2048,2048]{1,0:T(8,128)(2,1)}), bf16[512,2048]{1,0:T(8,128)(2,1)}) %reduce-scatter.11.cloned.1.call-update) | async-done | bytes 2097168 | tf_op jit(solution)/shard_map/reduce_scatter | solution.py:255
  1829.4 41.9 %all-reduce = (f32[]{:T(128)}, f32[64]{0:T(128)}, f32[64]{0:T(128)}, f32[2048]{0:T(1024)}, f32[2048]{0:T(1024)}) all-reduce(f32[]{:T(128)} %get-tuple-element.209, f32[64]{0:T(128)S(1)} %reduce_sum.176, f32[64]{0:T(128)S(1)} %get-tuple-element.212, ...), channel_id=1, replica_groups=mesh['dp'=8,'tensor'=4] {'dp','tensor'}, use_global_device_ids=true, to_apply=%region_11.12 | all-reduce | flops 4225 | bytes 33800 | tf_op jit(solution)/shard_map/psum | solution.py:191
  1878.2 97.6 %all-reduce.6.cloned.1.call-done = (f32[2048,256]{1,0:T(8,128)}, f32[2048,256]{1,0:T(8,128)}) async-done(((f32[2048,256]{1,0:T(8,128)}, f32[2048,256]{1,0:T(8,128)}), (f32[2048,256]{1,0:T(8,128)}, f32[2048,256]{1,0:T(8,128)})) %all-reduce.6.cloned.1.call-update) | async-done | bytes 4194320 | tf_op jit(solution)/shard_map/psum | solution.py:291
  (317 shorter events, 369.2 us)
Async XLA Ops:
  7.2 224.5 %copy-start = (bf16[256,2048]{1,0:T(8,128)(2,1)S(1)}, bf16[256,2048]{1,0:T(8,128)(2,1)}, u32[]{:S(2)}) copy-start(bf16[256,2048]{1,0:T(8,128)(2,1)} %param.28) | copy-start | bytes 3145732
  7.2 159.3 %all-gather.7.cloned.1.call-start = ((), (), s32[]{:S(2)}) async-start(), calls=%async_computation.4 | async-start | bytes 10485760 | tf_op jit(solution)/shard_map/all_gather | solution.py:140
  14.0 506.2 %reduce-scatter.5.cloned.1.call-start = ((), (), s32[]{:S(2)}) async-start(), calls=%async_computation.5 | async-start | bytes 20971520 | tf_op jit(solution)/shard_map/reduce_scatter | solution.py:170
  15.1 163.1 %copy-start.14 = (f32[8,8,2,1024]{3,1,2,0:T(8,128)}, f32[8,8,2,1024]{3,1,2,0:T(8,128)S(1)}, u32[]{:S(2)}) copy-start(f32[8,8,2,1024]{3,1,2,0:T(8,128)S(1)} %copy.130) | copy-start | bytes 1572868
  16.0 162.3 %copy-start.7 = (f32[8,8,2,1024]{3,1,2,0:T(8,128)}, f32[8,8,2,1024]{3,1,2,0:T(8,128)S(1)}, u32[]{:S(2)}) copy-start(f32[8,8,2,1024]{3,1,2,0:T(8,128)S(1)} %copy.129) | copy-start | bytes 1572868
  17.7 156.1 %copy-start.29 = (bf16[2048,64]{1,0:T(8,128)(2,1)}, bf16[2048,64]{1,0:T(8,128)(2,1)S(1)}, u32[]{:S(2)}) copy-start(bf16[2048,64]{1,0:T(8,128)(2,1)S(1)} %get-tuple-element.299) | copy-start | bytes 786436
  17.7 156.1 %copy-start.31 = (bf16[2048,64]{1,0:T(8,128)(2,1)}, bf16[2048,64]{1,0:T(8,128)(2,1)S(1)}, u32[]{:S(2)}) copy-start(bf16[2048,64]{1,0:T(8,128)(2,1)S(1)} %get-tuple-element.300) | copy-start | bytes 786436
  241.5 278.7 %copy-start.3 = (bf16[512,2048]{1,0:T(8,128)(2,1)S(1)}, bf16[512,2048]{1,0:T(8,128)(2,1)}, u32[]{:S(2)}) copy-start(bf16[512,2048]{1,0:T(8,128)(2,1)} %param.19) | copy-start | bytes 6291460
  241.5 284.6 %copy-start.37 = (f32[2048]{0:T(1024)S(1)}, f32[2048]{0:T(1024)}, u32[]{:S(2)}) copy-start(f32[2048]{0:T(1024)} %param.30) | copy-start | bytes 24580
  241.6 439.1 %all-gather.9.cloned.1.call-start = ((), (), s32[]{:S(2)}) async-start(), calls=%async_computation.6 | async-start | bytes 10485760 | tf_op jit(solution)/shard_map/all_gather | solution.py:178
  530.1 345.0 %reduce-scatter.7.cloned.1.call-start = ((), (), s32[]{:S(2)}) async-start(), calls=%async_computation.7 | async-start | bytes 10485760 | tf_op jit(solution)/shard_map/reduce_scatter | solution.py:183
  731.2 143.9 %copy-start.5 = (bf16[512,2048]{1,0:T(8,128)(2,1)S(1)}, bf16[512,2048]{1,0:T(8,128)(2,1)}, u32[]{:S(2)}) copy-start(bf16[512,2048]{1,0:T(8,128)(2,1)} %param.20) | copy-start | bytes 6291460
  731.3 299.8 %all-gather.11.cloned.1.call-start = ((), (), s32[]{:S(2)}) async-start(), calls=%async_computation.8 | async-start | bytes 10485760 | tf_op jit(solution)/shard_map/all_gather | solution.py:197
  880.5 354.9 %reduce-scatter.9.cloned.1.call-start = ((), (), s32[]{:S(2)}) async-start(), calls=%async_computation.9 | async-start | bytes 10485760 | tf_op jit(solution)/shard_map/reduce_scatter | solution.py:206
  1092.6 142.9 %copy-start.38 = (f32[2048]{0:T(1024)S(1)}, f32[2048]{0:T(1024)}, u32[]{:S(2)}) copy-start(f32[2048]{0:T(1024)} %param.30) | copy-start | bytes 24580
  1092.6 142.9 %copy-start.45 = (f32[512]{0:T(512)S(1)}, f32[512]{0:T(512)}, u32[]{:S(2)}) copy-start(f32[512]{0:T(512)} %copy-done.44) | copy-start | bytes 6148
  1092.6 148.7 %copy-start.49 = (f32[512]{0:T(512)S(1)}, f32[512]{0:T(512)}, u32[]{:S(2)}) copy-start(f32[512]{0:T(512)} %get-tuple-element.291) | copy-start | bytes 6148
  1092.6 305.5 %all-gather.13.cloned.1.call-start = ((), (), s32[]{:S(2)}) async-start(), calls=%async_computation.10 | async-start | bytes 10485760 | tf_op jit(solution)/shard_map/all_gather | solution.py:217
  1247.6 375.0 %all-reduce.8.cloned.1.call-start = ((), (), s32[]{:S(2)}) async-start(), calls=%async_computation.14 | async-start | bytes 33554432 | tf_op jit(solution)/shard_map/psum | solution.py:286
  1404.9 274.7 %all-gather.15.cloned.1.call-start = ((), (), s32[]{:S(2)}) async-start(), calls=%async_computation.12 | async-start | bytes 9437184 | tf_op jit(solution)/shard_map/all_gather | solution.py:285
  1564.8 261.4 %reduce-scatter.11.cloned.1.call-start = ((), (), s32[]{:S(2)}) async-start(), calls=%async_computation.11 | async-start | bytes 10485760 | tf_op jit(solution)/shard_map/reduce_scatter | solution.py:255
  1574.4 401.4 %all-reduce.6.cloned.1.call-start = ((), (), s32[]{:S(2)}) async-start(), calls=%async_computation.13 | async-start | bytes 8388608 | tf_op jit(solution)/shard_map/psum | solution.py:291
  1695.8 130.5 %copy-start.42 = (f32[512]{0:T(512)S(1)}, f32[512]{0:T(512)}, u32[]{:S(2)}) copy-start(f32[512]{0:T(512)} %copy-done.41) | copy-start | bytes 6148
  1707.2 164.8 %copy-start.52 = (f32[512]{0:T(512)S(1)}, f32[512]{0:T(512)}, u32[]{:S(2)}) copy-start(f32[512]{0:T(512)} %get-tuple-element.289) | copy-start | bytes 6148
  (61 other events, 881.4 us)
Sparse Core Ops, SparseCore 0:
  14.2 152.3 all-gather.6
  241.7 278.5 reduce-scatter.4
  530.2 150.3 all-gather.8
  731.4 143.6 reduce-scatter.6
  880.7 150.3 all-gather.10
  1092.7 142.6 reduce-scatter.8
  1247.7 150.3 all-gather.12
  1405.0 217.6 all-reduce.7
  1625.1 54.3 all-gather.14
  1681.8 144.4 reduce-scatter.10
  1832.6 143.1 all-reduce.5
